TPU v7x, 128 devices: a whole 4x4x4 slice. The times are simulated.
128 devices in a mesh: sec: 2 (over x_lo), batch: 32 (over z, y, core), head: 2 (over x_hi).
Axes of the slice: x: 4 (x_hi: 2, x_lo: 2; x = x_hi * 2 + x_lo), y: 4, z: 4, core: 2. Of those that a mesh axis runs over, the one named last changes fastest.
Arguments:
- hidden_in: bfloat16 [1024, 7168], P('batch'), may hold values from -6 to 6
- queries: bfloat16 [1024, 128, 576], P('batch', ('sec', 'head')), may hold values from -8 to 8
- latent_cache: bfloat16 [1024, 192, 576], P('batch'), may hold values from -8 to 8
- new_latent: bfloat16 [1024, 576], P('batch'), may hold values from -8 to 8
- cache_lengths: int32 [1024], P('batch'), may hold values from 1 to 192, 98304 in all
- value_up: bfloat16 [128, 512, 128], P(('sec', 'head')), may hold values from -0.25 to 0.25
- out_proj: bfloat16 [16384, 7168], P(('sec', 'head'), 'batch'), may hold values from -0.046875 to 0.046875
- norm_gain: float32 [7168], replicated, may hold values from 0.1 to 1.9
- router: bfloat16 [7168, 32], replicated, may hold values from -0.03125 to 0.03125
- expert_ids: int32 [1024, 8], P('batch'), may hold values from 0 to 31, all different within a row; in each aligned block of 32 rows (0 to 31, 32 to 63, ...) at most 16 rows name the same one
- w_gate_up: bfloat16 [32, 7168, 2, 1024], P('batch', None, None, ('sec', 'head')), may hold values from -0.0625 to 0.0625
- w_down: bfloat16 [32, 1024, 7168], P('batch', ('sec', 'head')), may hold values from -0.1875 to 0.1875
Outputs:
- mixed_out: bfloat16 [1024, 7168], P('batch', ('sec', 'head'))
Inputs may be any that keep to these rules, and one draw needn't show every extreme that they name: `expert_ids`: each row names 8 different experts. Among the 32 rows of one index of batch (aligned blocks) no expert is named by more than 16 rows, a bound that some block reaches. `cache_lengths`: the lengths of all rows add up to 98304, and one row has exactly 192.
All inputs are finite; a program needn't handle non-finite values. No bound on the sum of `cache_lengths` on one device may be relied on, other than what follows from the above.
Results may differ from a plain program's by a relative error of at most 0.007.
Values may be sent and summed in bfloat16 or wider, within the bound.
A program may use at most 128 MiB of HBM per device.

v0:
```python
import jax
import jax.numpy as jnp
from jax import lax
from jax.sharding import PartitionSpec as P

QKD = 192
TOP = 8
norm_epsilon = 1e-06
route_scale = 2.5


def body(
    hidden_in,
    queries,
    latent_cache,
    new_latent,
    cache_lengths,
    value_up,
    out_proj,
    norm_gain,
    router,
    expert_ids,
    w_gate_up,
    w_down,
):
    row_count = hidden_in.shape[0]
    model_width = hidden_in.shape[1]
    latent_width = value_up.shape[1]
    cache_depth = latent_cache.shape[1]
    group_count = lax.axis_size("batch")
    slice_count = lax.axis_size(("sec", "head"))
    slice_index = lax.axis_index(("sec", "head"))
    column_width = model_width // slice_count
    capacity = min(row_count, 2 * row_count * TOP // group_count)
    score_scale = QKD ** (-0.5)
    scores = (
        jnp.einsum("thk,tjk->thj", queries, latent_cache, preferred_element_type=jnp.float32)
        * score_scale
    )
    own_score = (
        jnp.einsum("thk,tk->th", queries, new_latent, preferred_element_type=jnp.float32)
        * score_scale
    )
    positions = lax.broadcasted_iota(jnp.int32, (1, 1, cache_depth), 2)
    in_cache = positions < cache_lengths[:, None, None]
    scores = jnp.where(in_cache, scores, -jnp.inf)
    top_score = jnp.maximum(jnp.max(scores, axis=2), own_score)
    cache_exp = jnp.exp(scores - top_score[:, :, None])
    own_exp = jnp.exp(own_score - top_score)
    softmax_sum = jnp.sum(cache_exp, axis=2) + own_exp
    cache_weights = (cache_exp / softmax_sum[:, :, None]).astype(jnp.bfloat16)
    own_weights = (own_exp / softmax_sum).astype(jnp.bfloat16)
    latent_out = jnp.einsum(
        "thj,tjc->thc",
        cache_weights,
        latent_cache[:, :, :latent_width],
        preferred_element_type=jnp.float32,
    )
    latent_out = latent_out + own_weights.astype(jnp.float32)[:, :, None] * new_latent[
        :, None, :latent_width
    ].astype(jnp.float32)
    latent_out = latent_out.astype(jnp.bfloat16)
    head_out = jnp.einsum(
        "thc,hcd->thd", latent_out, value_up, preferred_element_type=jnp.float32
    ).astype(jnp.bfloat16)
    head_out = head_out.reshape(row_count, -1)
    column_part = jnp.dot(
        lax.all_gather(head_out, "batch", axis=0, tiled=True),
        out_proj,
        preferred_element_type=jnp.float32,
    )
    row_part = lax.all_to_all(column_part, "batch", split_axis=0, concat_axis=1, tiled=True)
    attention = lax.psum(row_part, ("sec", "head"))
    residual = hidden_in.astype(jnp.float32) + attention
    mean_square = jnp.mean(residual * residual, axis=1, keepdims=True)
    normed = (residual * lax.rsqrt(mean_square + norm_epsilon) * norm_gain).astype(jnp.bfloat16)
    logits = jnp.dot(normed, router, preferred_element_type=jnp.float32)
    affinity = jax.nn.sigmoid(logits)
    expert_grid = lax.broadcasted_iota(jnp.int32, (1, 1, group_count), 2)
    hit_table = expert_ids[:, :, None] == expert_grid
    picked = jnp.sum(jnp.where(hit_table, affinity[:, None, :], 0.0), axis=2)
    route_weights = route_scale * picked / jnp.sum(picked, axis=1, keepdims=True)
    flat_hits = hit_table.reshape(row_count * TOP, group_count).astype(jnp.int32)
    earlier = jnp.cumsum(flat_hits, axis=0) - flat_hits
    slot_index = jnp.sum(earlier * flat_hits, axis=1)
    position = expert_ids.reshape(-1) * capacity + slot_index
    buffer_grid = lax.broadcasted_iota(jnp.int32, (1, group_count * capacity), 1)
    place_table = (position[:, None] == buffer_grid).astype(jnp.bfloat16)
    dispatch_table = jnp.sum(place_table.reshape(row_count, TOP, group_count * capacity), axis=1)
    gate_up_weight = w_gate_up[0].reshape(model_width, -1)
    hidden_share = w_down.shape[1]
    outgoing = jnp.einsum("rs,rd->sd", dispatch_table, normed, preferred_element_type=jnp.float32)
    outgoing = outgoing.astype(jnp.bfloat16).reshape(group_count, capacity, model_width)
    arrived = lax.all_to_all(outgoing, "batch", split_axis=0, concat_axis=0, tiled=True)
    flat_in = arrived.reshape(-1, model_width)
    gate_up = jnp.dot(flat_in, gate_up_weight, preferred_element_type=jnp.float32)
    activated = (jax.nn.silu(gate_up[:, :hidden_share]) * gate_up[:, hidden_share:]).astype(
        jnp.bfloat16
    )
    result = jnp.dot(activated, w_down[0], preferred_element_type=jnp.float32)
    partial_out = result.reshape(arrived.shape[0], arrived.shape[1], model_width)
    summed_out = lax.psum_scatter(partial_out, ("sec", "head"), scatter_dimension=2, tiled=True)
    returned = lax.all_to_all(summed_out, "batch", split_axis=0, concat_axis=0, tiled=True)
    flat_back = returned.reshape(group_count * capacity, column_width)
    gathered = flat_back[position].reshape(row_count, TOP, column_width)
    mixture = jnp.sum(gathered * route_weights[:, :, None], axis=1)
    residual_cols = lax.dynamic_slice_in_dim(residual, slice_index * column_width, column_width, 1)
    return (residual_cols + mixture).astype(jnp.bfloat16)


def solution(mesh):
    in_specs = (
        P("batch", None),
        P("batch", ("sec", "head"), None),
        P("batch", None, None),
        P("batch", None),
        P("batch"),
        P(("sec", "head"), None, None),
        P(("sec", "head"), "batch"),
        P(),
        P(),
        P("batch", None),
        P("batch", None, None, ("sec", "head")),
        P("batch", ("sec", "head"), None),
    )
    out_specs = P("batch", ("sec", "head"))
    return jax.shard_map(body, mesh=mesh, in_specs=in_specs, out_specs=out_specs, check_vma=False)
```

profile of v0, /device:TPU:0, one launch (start us, length us, event | category | flops | bytes accessed | tf_op | source)
XLA Modules:
  0.0 588.6 jit_solution(7912476928784417901)
XLA Ops:
  6.5 0.9 iota_compare_fusion.4
  7.4 0.8 slice_convert_fusion
  8.2 1.8 fusion.19
  10.0 6.8 %fusion.28 = (f32[32,32]{1,0:T(8,128)S(1)}, f32[32,32,192]{2,1,0:T(8,128)S(1)}) fusion(bf16[32,32,576]{2,1,0:T(8,128)(2,1)} %param.13, bf16[32,192,576]{2,1,0:T(8,128)(2,1)} %param.14, pred[32,192]{1,0:T(8,128)(4,1)S(1)} %iota_compare_fusion.4), kind=kOutput, calls=%fused_computation.60 | convolution fusion | flops 227081216 | bytes 9054208 | tf_op jit(solution)/shard_map/thk,tjk->thj/dot_general | solution.py:37
  17.2 1.5 add_convert_fusion
  19.4 1.1 fusion.8
  20.5 0.8 copy.55
  21.3 55.6 %all-gather.2.cloned.1.call-done = bf16[1024,4096]{1,0:T(8,128)(2,1)} async-done(((bf16[32,4096]{1,0:T(8,128)(2,1)}), bf16[1024,4096]{1,0:T(8,128)(2,1)}) %all-gather.2.cloned.1.call-update) | async-done | bytes 8388624 | tf_op jit(solution)/shard_map/all_gather | solution.py:68
  76.9 5.7 fusion.29
  82.7 22.8 %all_to_all.29 = f32[32,32,224]{2,1,0:T(8,128)S(1)} all-to-all(f32[32,32,224]{2,1,0:T(8,128)S(1)} %bitcast.63), channel_id=1, replica_groups=mesh['sec'=2,'batch'=32,'head'=2] {'batch'}, dimensions={0} | all-to-all | bytes 1835008 | tf_op jit(solution)/shard_map/all_to_all | solution.py:72
  106.0 1.6 all_to_all.23
  109.2 41.3 %all-reduce.2.cloned.1.call-done = f32[32,7168]{1,0:T(8,128)} async-done(((f32[32,7168]{1,0:T(8,128)}), f32[32,7168]{1,0:T(8,128)}) %all-reduce.2.cloned.1.call-update) | async-done | bytes 917520 | tf_op jit(solution)/shard_map/psum | solution.py:73
  150.5 1.4 multiply_reduce_fusion
  151.9 5.1 convolution_convert_fusion
  157.1 7.4 %all-to-all-start.1 = ((bf16[32,16,7168]{2,1,0:T(8,128)(2,1)}), bf16[32,16,7168]{2,1,0:T(8,128)(2,1)}, u32[]{:S(2)}, u32[]{:S(2)}) async-start(bf16[32,16,7168]{2,1,0:T(8,128)(2,1)} %bitcast.58), calls=%async_computation.1 | async-start | bytes 14680064 | tf_op jit(solution)/shard_map/all_to_all | solution.py:94
  164.7 7.3 %copy.48 = bf16[896,8,2,256]{3,1,2,0:T(8,128)(2,1)} copy(bf16[896,8,2,256]{3,2,1,0:T(2,128)(2,1)} %bitcast.59) | data formatting | bytes 14680064
  172.0 84.8 %all-to-all-done.1 = bf16[32,16,7168]{2,1,0:T(8,128)(2,1)} async-done(((bf16[32,16,7168]{2,1,0:T(8,128)(2,1)}), bf16[32,16,7168]{2,1,0:T(8,128)(2,1)}, u32[]{:S(2)}, u32[]{:S(2)}) %all-to-all-start.1) | async-done | bytes 7340064 | tf_op jit(solution)/shard_map/all_to_all | solution.py:94
  256.8 8.6 %fusion.30 = f32[512,512]{1,0:T(8,128)S(1)} fusion(bf16[512,7168]{1,0:T(8,128)(2,1)} %bitcast.8, bf16[7168,512]{1,0:T(8,128)(2,1)} %bitcast.60), kind=kOutput, calls=%fused_computation.62 | convolution fusion | flops 3758096384 | bytes 15728640 | tf_op jit(solution)/shard_map/dot_general | solution.py:96
  265.5 7.3 %fusion.2 = f32[32,16,7168]{2,1,0:T(8,128)} fusion(bf16[32,16,256]{2,1,0:T(8,128)(2,1)S(1)} %bitcast.62, bf16[1,256,7168]{2,1,0:T(8,128)(2,1)S(1)} %copy-done.4), kind=kOutput, calls=%fused_computation.4 | convolution fusion | flops 1879048192 | bytes 18612224 | tf_op jit(solution)/shard_map/dot_general | solution.py:100
  272.9 245.9 %reduce-scatter.2.cloned.1.call-done = f32[32,16,1792]{2,1,0:T(8,128)} async-done(((f32[32,16,7168]{2,1,0:T(8,128)}), f32[32,16,1792]{2,1,0:T(8,128)}) %reduce-scatter.2.cloned.1.call-update) | async-done | bytes 3670032 | tf_op jit(solution)/shard_map/reduce_scatter | solution.py:102
  518.7 7.4 %all-to-all-start.2 = ((f32[32,16,1792]{2,1,0:T(8,128)}), f32[32,16,1792]{2,1,0:T(8,128)}, u32[]{:S(2)}, u32[]{:S(2)}) async-start(f32[32,16,1792]{2,1,0:T(8,128)} %reduce-scatter.2.cloned.1.call-done), calls=%async_computation.3 | async-start | bytes 7340032 | tf_op jit(solution)/shard_map/all_to_all | solution.py:103
  527.2 46.6 %all-to-all-done.2 = f32[32,16,1792]{2,1,0:T(8,128)} async-done(((f32[32,16,1792]{2,1,0:T(8,128)}), f32[32,16,1792]{2,1,0:T(8,128)}, u32[]{:S(2)}, u32[]{:S(2)}) %all-to-all-start.2) | async-done | bytes 3670048 | tf_op jit(solution)/shard_map/all_to_all | solution.py:103
  573.8 5.5 gather_fusion
  579.3 2.1 fusion.4
  (49 shorter events, 5.4 us)
Async XLA Ops:
  6.5 70.3 %copy-start = (bf16[4096,224]{0,1:T(8,128)(2,1)S(1)}, bf16[4096,224]{0,1:T(8,128)(2,1)}, u32[]{:S(2)}) copy-start(bf16[4096,224]{0,1:T(8,128)(2,1)} %param.18) | copy-start | bytes 5505028
  6.5 70.3 %all-gather.2.cloned.1.call-start = ((), (), s32[]{:S(2)}) async-start(), calls=%async_computation.4 | async-start | bytes 8650752 | tf_op jit(solution)/shard_map/all_gather | solution.py:68
  10.0 7.2 %copy-start.2 = (bf16[32,192,576]{2,1,0:T(8,128)(2,1)S(1)}, bf16[32,192,576]{2,1,0:T(8,128)(2,1)}, u32[]{:S(2)}) copy-start(bf16[32,192,576]{2,1,0:T(8,128)(2,1)} %param.14) | copy-start | bytes 21233668
  17.2 2.2 copy-start.3
  21.2 129.3 %all-reduce.2.cloned.1.call-start = ((), (), s32[]{:S(2)}) async-start(), calls=%async_computation.5 | async-start | bytes 1835008 | tf_op jit(solution)/shard_map/psum | solution.py:73
  82.6 25.0 %copy-start.8 = (s32[32,8]{0,1:T(8,128)S(1)}, s32[32,8]{0,1:T(8,128)}, u32[]{:S(2)}) copy-start(s32[32,8]{0,1:T(8,128)} %param.21) | copy-start | bytes 3076
  82.6 67.9 %copy-start.5 = (bf16[32,7168]{1,0:T(8,128)(2,1)S(1)}, bf16[32,7168]{1,0:T(8,128)(2,1)}, u32[]{:S(2)}) copy-start(bf16[32,7168]{1,0:T(8,128)(2,1)} %param.12) | copy-start | bytes 1376260
  105.4 46.5 %copy-start.7 = (f32[7168]{0:T(1024)S(1)}, f32[7168]{0:T(1024)}, u32[]{:S(2)}) copy-start(f32[7168]{0:T(1024)} %param.19) | copy-start | bytes 86020
  157.1 99.7 %all-to-all-start.1 = ((bf16[32,16,7168]{2,1,0:T(8,128)(2,1)}), bf16[32,16,7168]{2,1,0:T(8,128)(2,1)}, u32[]{:S(2)}, u32[]{:S(2)}) async-start(bf16[32,16,7168]{2,1,0:T(8,128)(2,1)} %bitcast.58), calls=%async_computation.1 | async-start | bytes 14680064 | tf_op jit(solution)/shard_map/all_to_all | solution.py:94
  164.5 354.3 %reduce-scatter.2.cloned.1.call-start = ((), (), s32[]{:S(2)}) async-start(), calls=%async_computation.6 | async-start | bytes 18350080 | tf_op jit(solution)/shard_map/reduce_scatter | solution.py:102
  256.8 8.8 %copy-start.4 = (bf16[1,256,7168]{2,1,0:T(8,128)(2,1)S(1)}, bf16[1,256,7168]{2,1,0:T(8,128)(2,1)}, u32[]{:S(2)}) copy-start(bf16[1,256,7168]{2,1,0:T(8,128)(2,1)} %param.23) | copy-start | bytes 11010052
  272.8 253.4 %copy-start.6 = (bf16[7168,32]{0,1:T(8,128)(2,1)S(1)}, bf16[7168,32]{0,1:T(8,128)(2,1)}, u32[]{:S(2)}) copy-start(bf16[7168,32]{0,1:T(8,128)(2,1)} %param.20) | copy-start | bytes 1376260
  518.7 55.1 %all-to-all-start.2 = ((f32[32,16,1792]{2,1,0:T(8,128)}), f32[32,16,1792]{2,1,0:T(8,128)}, u32[]{:S(2)}, u32[]{:S(2)}) async-start(f32[32,16,1792]{2,1,0:T(8,128)} %reduce-scatter.2.cloned.1.call-done), calls=%async_computation.3 | async-start | bytes 7340032 | tf_op jit(solution)/shard_map/all_to_all | solution.py:103
  573.8 8.3 %copy-start.1 = (bf16[4096,224]{0,1:T(8,128)(2,1)S(1)}, bf16[4096,224]{0,1:T(8,128)(2,1)}, u32[]{:S(2)}) copy-start(bf16[4096,224]{0,1:T(8,128)(2,1)} %param.18) | copy-start | bytes 5505028
Sparse Core Ops, SparseCore 0:
  21.4 55.4 all-gather.1
  107.8 42.6 all-reduce.1
  273.0 245.7 reduce-scatter.1
where the time goes:
time: 589 us
  waiting for transfers between devices  474 us (80%)
  matrix products  38.3 us (7%)
  blocking collectives  22.8 us (4%)
  local copies, waits for them, and re-layouts  17.1 us (3%)
  starting transfers between devices  15 us (3%)
  between operations  13.3 us (2%)
  other arithmetic  7.99 us (1%)
    reduce_scatter x1, waiting for transfers between devices, body(): lax.psum_scatter(partial_out, ('sec', 'head'), scatter_dimension=2, tiled...  246 us
    all_to_all x1, waiting for transfers between devices, body(): lax.all_to_all(outgoing, 'batch', split_axis=0, concat_axis=0, tiled=True)  84.8 us
    all_gather x1, waiting for transfers between devices, body(): lax.all_gather(head_out, 'batch', axis=0, tiled=True)  55.6 us
    all_to_all x1, waiting for transfers between devices, body(): lax.all_to_all(summed_out, 'batch', split_axis=0, concat_axis=0, tiled=True)  46.6 us
    psum x1, waiting for transfers between devices, body(): attention = lax.psum(row_part, ('sec', 'head'))  41.3 us
    all_to_all x1, blocking collectives, body(): lax.all_to_all(column_part, 'batch', split_axis=0, concat_axis=1, tiled=T...  22.8 us
  transfers between devices with their start and end apart: 5, of which 5 were waited for; matrix products, arithmetic and copies ran while one was open for 2% of the time, Pallas kernels for 0%

commit v1 on v0

--- a/solution.py
+++ b/solution.py
@@ -70,7 +70,7 @@
         preferred_element_type=jnp.float32,
     )
     row_part = lax.all_to_all(column_part, "batch", split_axis=0, concat_axis=1, tiled=True)
-    attention = lax.psum(row_part, ("sec", "head"))
+    attention = lax.psum(lax.psum(row_part, "head"), "sec")
     residual = hidden_in.astype(jnp.float32) + attention
     mean_square = jnp.mean(residual * residual, axis=1, keepdims=True)
     normed = (residual * lax.rsqrt(mean_square + norm_epsilon) * norm_gain).astype(jnp.bfloat16)

time: 589 us -> 635 us (1.078)
  waiting for transfers between devices: 474 us -> 520 us
    psum x1 -> x2, waiting for transfers between devices: 41.3 us -> 87.2 us  [body(): attention = lax.psum(lax.psum(row_part, 'head'), 'sec')]
  transfers between devices with their start and end apart: 5 -> 6, of which waited for: 5 -> 6; matrix products, arithmetic and copies ran while one was open for 2% -> 2% of each run, Pallas kernels for 0% -> 0%
where the time goes in v1:
time: 635 us
  waiting for transfers between devices  520 us (82%)
  matrix products  38.3 us (6%)
  blocking collectives  22.8 us (4%)
  local copies, waits for them, and re-layouts  17.1 us (3%)
  starting transfers between devices  15.1 us (2%)
  between operations  13.4 us (2%)
  other arithmetic  7.99 us (1%)
    reduce_scatter x1, waiting for transfers between devices, body(): lax.psum_scatter(partial_out, ('sec', 'head'), scatter_dimension=2, tiled...  246 us
    psum x2, waiting for transfers between devices, body(): attention = lax.psum(lax.psum(row_part, 'head'), 'sec')  87.2 us
    all_to_all x1, waiting for transfers between devices, body(): lax.all_to_all(outgoing, 'batch', split_axis=0, concat_axis=0, tiled=True)  84.8 us
    all_gather x1, waiting for transfers between devices, body(): lax.all_gather(head_out, 'batch', axis=0, tiled=True)  55.6 us
    all_to_all x1, waiting for transfers between devices, body(): lax.all_to_all(summed_out, 'batch', split_axis=0, concat_axis=0, tiled=True)  46.6 us
    all_to_all x1, blocking collectives, body(): lax.all_to_all(column_part, 'batch', split_axis=0, concat_axis=1, tiled=T...  22.8 us
  transfers between devices with their start and end apart: 6, of which 6 were waited for; matrix products, arithmetic and copies ran while one was open for 2% of the time, Pallas kernels for 0%

profile of v1, /device:TPU:0, one launch (start us, length us, event | category | flops | bytes accessed | tf_op | source)
XLA Modules:
  0.0 634.7 jit_solution(5968680274094345689)
XLA Ops:
  6.5 0.9 iota_compare_fusion.4
  7.4 0.8 slice_convert_fusion
  8.2 1.8 fusion.19
  10.0 6.8 %fusion.28 = (f32[32,32]{1,0:T(8,128)S(1)}, f32[32,32,192]{2,1,0:T(8,128)S(1)}) fusion(bf16[32,32,576]{2,1,0:T(8,128)(2,1)} %param.13, bf16[32,192,576]{2,1,0:T(8,128)(2,1)} %param.14, pred[32,192]{1,0:T(8,128)(4,1)S(1)} %iota_compare_fusion.4), kind=kOutput, calls=%fused_computation.60 | convolution fusion | flops 227081216 | bytes 9054208 | tf_op jit(solution)/shard_map/thk,tjk->thj/dot_general | solution.py:37
  17.2 1.5 add_convert_fusion
  19.4 1.1 fusion.8
  21.3 55.6 %all-gather.2.cloned.1.call-done = bf16[1024,4096]{1,0:T(8,128)(2,1)} async-done(((bf16[32,4096]{1,0:T(8,128)(2,1)}), bf16[1024,4096]{1,0:T(8,128)(2,1)}) %all-gather.2.cloned.1.call-update) | async-done | bytes 8388624 | tf_op jit(solution)/shard_map/all_gather | solution.py:68
  76.9 5.7 fusion.29
  82.7 22.8 %all_to_all.29 = f32[32,32,224]{2,1,0:T(8,128)S(1)} all-to-all(f32[32,32,224]{2,1,0:T(8,128)S(1)} %bitcast.63), channel_id=1, replica_groups=mesh['sec'=2,'batch'=32,'head'=2] {'batch'}, dimensions={0} | all-to-all | bytes 1835008 | tf_op jit(solution)/shard_map/all_to_all | solution.py:72
  106.0 1.6 all_to_all.23
  107.7 43.0 %all-reduce.3.cloned.1.call-done = f32[32,7168]{1,0:T(8,128)} async-done(((f32[32,7168]{1,0:T(8,128)}), f32[32,7168]{1,0:T(8,128)}) %all-reduce.3.cloned.1.call-update) | async-done | bytes 917520 | tf_op jit(solution)/shard_map/psum | solution.py:73
  152.2 44.3 %all-reduce.5.cloned.1.call-done = f32[32,7168]{1,0:T(8,128)} async-done(((f32[32,7168]{1,0:T(8,128)}), f32[32,7168]{1,0:T(8,128)}) %all-reduce.5.cloned.1.call-update) | async-done | bytes 917520 | tf_op jit(solution)/shard_map/psum | solution.py:73
  196.5 1.4 multiply_reduce_fusion
  197.9 5.1 convolution_convert_fusion
  203.1 7.4 %all-to-all-start.1 = ((bf16[32,16,7168]{2,1,0:T(8,128)(2,1)}), bf16[32,16,7168]{2,1,0:T(8,128)(2,1)}, u32[]{:S(2)}, u32[]{:S(2)}) async-start(bf16[32,16,7168]{2,1,0:T(8,128)(2,1)} %bitcast.58), calls=%async_computation.1 | async-start | bytes 14680064 | tf_op jit(solution)/shard_map/all_to_all | solution.py:94
  210.7 7.3 %copy.48 = bf16[896,8,2,256]{3,1,2,0:T(8,128)(2,1)} copy(bf16[896,8,2,256]{3,2,1,0:T(2,128)(2,1)} %bitcast.59) | data formatting | bytes 14680064
  218.0 84.8 %all-to-all-done.1 = bf16[32,16,7168]{2,1,0:T(8,128)(2,1)} async-done(((bf16[32,16,7168]{2,1,0:T(8,128)(2,1)}), bf16[32,16,7168]{2,1,0:T(8,128)(2,1)}, u32[]{:S(2)}, u32[]{:S(2)}) %all-to-all-start.1) | async-done | bytes 7340064 | tf_op jit(solution)/shard_map/all_to_all | solution.py:94
  302.8 8.6 %fusion.30 = f32[512,512]{1,0:T(8,128)S(1)} fusion(bf16[512,7168]{1,0:T(8,128)(2,1)} %bitcast.8, bf16[7168,512]{1,0:T(8,128)(2,1)} %bitcast.60), kind=kOutput, calls=%fused_computation.62 | convolution fusion | flops 3758096384 | bytes 15728640 | tf_op jit(solution)/shard_map/dot_general | solution.py:96
  311.5 7.3 %fusion.2 = f32[32,16,7168]{2,1,0:T(8,128)} fusion(bf16[32,16,256]{2,1,0:T(8,128)(2,1)S(1)} %bitcast.62, bf16[1,256,7168]{2,1,0:T(8,128)(2,1)S(1)} %copy-done.4), kind=kOutput, calls=%fused_computation.4 | convolution fusion | flops 1879048192 | bytes 18612224 | tf_op jit(solution)/shard_map/dot_general | solution.py:100
  318.9 245.9 %reduce-scatter.2.cloned.1.call-done = f32[32,16,1792]{2,1,0:T(8,128)} async-done(((f32[32,16,7168]{2,1,0:T(8,128)}), f32[32,16,1792]{2,1,0:T(8,128)}) %reduce-scatter.2.cloned.1.call-update) | async-done | bytes 3670032 | tf_op jit(solution)/shard_map/reduce_scatter | solution.py:102
  564.8 7.4 %all-to-all-start.2 = ((f32[32,16,1792]{2,1,0:T(8,128)}), f32[32,16,1792]{2,1,0:T(8,128)}, u32[]{:S(2)}, u32[]{:S(2)}) async-start(f32[32,16,1792]{2,1,0:T(8,128)} %reduce-scatter.2.cloned.1.call-done), calls=%async_computation.3 | async-start | bytes 7340032 | tf_op jit(solution)/shard_map/all_to_all | solution.py:103
  573.2 46.6 %all-to-all-done.2 = f32[32,16,1792]{2,1,0:T(8,128)} async-done(((f32[32,16,1792]{2,1,0:T(8,128)}), f32[32,16,1792]{2,1,0:T(8,128)}, u32[]{:S(2)}, u32[]{:S(2)}) %all-to-all-start.2) | async-done | bytes 3670048 | tf_op jit(solution)/shard_map/all_to_all | solution.py:103
  619.8 5.5 gather_fusion
  625.3 2.1 fusion.4
  (52 shorter events, 6.2 us)
Async XLA Ops:
  6.5 70.3 %copy-start = (bf16[4096,224]{0,1:T(8,128)(2,1)S(1)}, bf16[4096,224]{0,1:T(8,128)(2,1)}, u32[]{:S(2)}) copy-start(bf16[4096,224]{0,1:T(8,128)(2,1)} %param.18) | copy-start | bytes 5505028
  6.5 70.3 %all-gather.2.cloned.1.call-start = ((), (), s32[]{:S(2)}) async-start(), calls=%async_computation.4 | async-start | bytes 8650752 | tf_op jit(solution)/shard_map/all_gather | solution.py:68
  10.0 7.2 %copy-start.2 = (bf16[32,192,576]{2,1,0:T(8,128)(2,1)S(1)}, bf16[32,192,576]{2,1,0:T(8,128)(2,1)}, u32[]{:S(2)}) copy-start(bf16[32,192,576]{2,1,0:T(8,128)(2,1)} %param.14) | copy-start | bytes 21233668
  17.2 2.2 copy-start.3
  21.2 129.4 %all-reduce.3.cloned.1.call-start = ((), (), s32[]{:S(2)}) async-start(), calls=%async_computation.5 | async-start | bytes 1835008 | tf_op jit(solution)/shard_map/psum | solution.py:73
  82.6 68.1 %copy-start.8 = (s32[32,8]{0,1:T(8,128)S(1)}, s32[32,8]{0,1:T(8,128)}, u32[]{:S(2)}) copy-start(s32[32,8]{0,1:T(8,128)} %param.21) | copy-start | bytes 3076
  82.6 113.9 %copy-start.5 = (bf16[32,7168]{1,0:T(8,128)(2,1)S(1)}, bf16[32,7168]{1,0:T(8,128)(2,1)}, u32[]{:S(2)}) copy-start(bf16[32,7168]{1,0:T(8,128)(2,1)} %param.12) | copy-start | bytes 1376260
  105.4 92.5 %copy-start.7 = (f32[7168]{0:T(1024)S(1)}, f32[7168]{0:T(1024)}, u32[]{:S(2)}) copy-start(f32[7168]{0:T(1024)} %param.19) | copy-start | bytes 86020
  107.6 88.8 %all-reduce.5.cloned.1.call-start = ((), (), s32[]{:S(2)}) async-start(), calls=%async_computation.6 | async-start | bytes 1835008 | tf_op jit(solution)/shard_map/psum | solution.py:73
  203.1 99.7 %all-to-all-start.1 = ((bf16[32,16,7168]{2,1,0:T(8,128)(2,1)}), bf16[32,16,7168]{2,1,0:T(8,128)(2,1)}, u32[]{:S(2)}, u32[]{:S(2)}) async-start(bf16[32,16,7168]{2,1,0:T(8,128)(2,1)} %bitcast.58), calls=%async_computation.1 | async-start | bytes 14680064 | tf_op jit(solution)/shard_map/all_to_all | solution.py:94
  210.5 354.3 %reduce-scatter.2.cloned.1.call-start = ((), (), s32[]{:S(2)}) async-start(), calls=%async_computation.7 | async-start | bytes 18350080 | tf_op jit(solution)/shard_map/reduce_scatter | solution.py:102
  302.8 8.8 %copy-start.4 = (bf16[1,256,7168]{2,1,0:T(8,128)(2,1)S(1)}, bf16[1,256,7168]{2,1,0:T(8,128)(2,1)}, u32[]{:S(2)}) copy-start(bf16[1,256,7168]{2,1,0:T(8,128)(2,1)} %param.23) | copy-start | bytes 11010052
  318.9 253.4 %copy-start.6 = (bf16[7168,32]{0,1:T(8,128)(2,1)S(1)}, bf16[7168,32]{0,1:T(8,128)(2,1)}, u32[]{:S(2)}) copy-start(bf16[7168,32]{0,1:T(8,128)(2,1)} %param.20) | copy-start | bytes 1376260
  564.8 55.1 %all-to-all-start.2 = ((f32[32,16,1792]{2,1,0:T(8,128)}), f32[32,16,1792]{2,1,0:T(8,128)}, u32[]{:S(2)}, u32[]{:S(2)}) async-start(f32[32,16,1792]{2,1,0:T(8,128)} %reduce-scatter.2.cloned.1.call-done), calls=%async_computation.3 | async-start | bytes 7340032 | tf_op jit(solution)/shard_map/all_to_all | solution.py:103
  619.8 8.3 %copy-start.1 = (bf16[4096,224]{0,1:T(8,128)(2,1)S(1)}, bf16[4096,224]{0,1:T(8,128)(2,1)}, u32[]{:S(2)}) copy-start(bf16[4096,224]{0,1:T(8,128)(2,1)} %param.18) | copy-start | bytes 5505028
Sparse Core Ops, SparseCore 0:
  21.4 55.4 all-gather.1
  107.8 42.8 all-reduce.2
  153.3 43.1 all-reduce.4
  319.0 245.7 reduce-scatter.1
